TPU v7x, 128 devices: a whole 4x4x4 slice. The times are simulated.
128 devices in a mesh: variant: 8 (over z_lo, x), vocab: 16 (over y, z_hi, core).
Axes of the slice: x: 4, y: 4, z: 4 (z_hi: 2, z_lo: 2; z = z_hi * 2 + z_lo), core: 2. Of those that a mesh axis runs over, the one named last changes fastest.
Arguments:
- teacher_hidden: bfloat16 [8, 256, 4096], P(None, None, ('variant', 'vocab')), may hold values from -24 to 24
- teacher_weight: bfloat16 [4096, 64128], P(None, ('vocab', 'variant')), may hold values from -1 to 1
- variant_ids: int32 [8], replicated, may hold values from 0 to 13
- temps: float32 [14], replicated, may hold values from 0.7 to 1.5
- student_hidden: bfloat16 [256, 2048], P(None, 'variant'), may hold values from -24 to 24
- student_weight: bfloat16 [2048, 64128], P('variant', 'vocab'), may hold values from -1 to 1
- token_ids: int32 [256], P('variant'), may hold values from 0 to 64127
- loss_mask: int32 [256], P('variant'), may hold values 0 or 1
Outputs:
- token_loss: float32 [256], P('variant')
- student_grad: float32 [2048, 64128], P('variant', 'vocab')
All inputs are finite; a program needn't handle non-finite values. No bound on the sum of `loss_mask` on one device may be relied on, other than what follows from the above.
Results may differ from a plain program's by a relative error of at most 0.0025.
Values may be sent and summed in bfloat16 or wider, within the bound.
No kernel may reach another device: no remote copies, remote signals or barrier semaphores. Data moves between devices by JAX's collectives and lax.ppermute only.
A program may use at most 192 MiB of HBM per device.

v0:
```python
import jax
import jax.numpy as jnp
from jax import lax
from jax.sharding import PartitionSpec as P

mix_weight = 0.5
loss_scale = 4096.0


def on_device(
    teacher_hidden,
    teacher_weight,
    variant_ids,
    temps,
    student_hidden,
    student_weight,
    token_ids,
    loss_mask,
):
    n_variant = lax.axis_size("variant")
    categories = jnp.arange(temps.shape[0], dtype=jnp.int32)
    taus = jnp.sum(
        jnp.where(variant_ids[:, None] == categories[None, :], temps[None, :], 0.0), axis=1
    )
    hidden_all = lax.all_gather(teacher_hidden, ("variant", "vocab"), axis=2, tiled=True)
    scaled = (
        jnp.einsum("vtd,dc->vtc", hidden_all, teacher_weight, preferred_element_type=jnp.float32)
        / taus[:, None, None]
    )
    local_max = jnp.max(scaled, axis=2)
    top = lax.pmax(local_max, ("variant", "vocab"))
    total = lax.psum(jnp.sum(jnp.exp(scaled - top[:, :, None]), axis=2), ("variant", "vocab"))
    probs = jnp.exp(scaled - top[:, :, None]) / total[:, :, None]
    averaged_cols = jnp.sum(probs, axis=0) / n_variant
    averaged = lax.all_to_all(
        averaged_cols.astype(jnp.bfloat16), "variant", split_axis=0, concat_axis=1, tiled=True
    ).astype(averaged_cols.dtype)
    block = student_hidden
    logits = lax.psum_scatter(
        jnp.dot(block, student_weight, preferred_element_type=jnp.float32),
        "variant",
        scatter_dimension=0,
        tiled=True,
    )
    local_max = jnp.max(logits, axis=1)
    top = lax.pmax(local_max, "vocab")
    total = lax.psum(jnp.sum(jnp.exp(logits - top[:, None]), axis=1), "vocab")
    log_probs = logits - (top + jnp.log(total))[:, None]
    probs_student = jnp.exp(log_probs)
    columns = lax.axis_index("vocab") * logits.shape[1] + jnp.arange(
        logits.shape[1], dtype=jnp.int32
    )
    onehot = token_ids[:, None] == columns[None, :]
    soft, hard = lax.psum(
        (jnp.sum(averaged * log_probs, axis=1), jnp.sum(jnp.where(onehot, log_probs, 0.0), axis=1)),
        "vocab",
    )
    maskf = loss_mask.astype(jnp.float32)
    token_loss = maskf * (-mix_weight * soft - (1.0 - mix_weight) * hard)
    error = (
        loss_scale
        * maskf[:, None]
        * (probs_student - mix_weight * averaged - (1.0 - mix_weight) * onehot.astype(jnp.float32))
    ).astype(jnp.bfloat16)
    block = student_hidden
    student_grad = lax.dot_general(
        block,
        lax.all_gather(error, "variant", axis=0, tiled=True),
        (((0,), (0,)), ((), ())),
        preferred_element_type=jnp.float32,
    )
    return (token_loss, student_grad)


def solution(mesh):
    in_specs = (
        P(None, None, ("variant", "vocab")),
        P(None, ("vocab", "variant")),
        P(),
        P(),
        P(None, "variant"),
        P("variant", "vocab"),
        P("variant"),
        P("variant"),
    )
    out_specs = (P("variant"), P("variant", "vocab"))
    return jax.shard_map(
        on_device, mesh=mesh, in_specs=in_specs, out_specs=out_specs, check_vma=False
    )
```

profile of v0, /device:TPU:0, one launch (start us, length us, event | category | flops | bytes accessed | tf_op | source)
XLA Modules:
  0.0 505.8 jit_solution(16824957268856968234)
XLA Ops:
  8.0 0.0 copy-start
  8.0 0.0 reduce-scatter.2.cloned.1.call-start
  8.1 1.5 copy-done
  9.6 3.6 fusion.11
  13.2 0.0 reduce-scatter.2.cloned.1.call-update
  13.2 0.0 all-gather.3.cloned.1.call-start
  13.2 0.5 all-gather.3.cloned.1.call-update
  13.8 0.2 select_reduce_fusion
  14.0 60.6 %reduce-scatter.2.cloned.1.call-done = f32[32,4008]{1,0:T(8,128)} async-done(((f32[256,4008]{1,0:T(8,128)}), f32[32,4008]{1,0:T(8,128)}) %reduce-scatter.2.cloned.1.call-update) | async-done | bytes 513040 | tf_op jit(solution)/shard_map/reduce_scatter | solution.py:39
  74.6 1.2 reduce_max.19
  75.8 38.9 %pmax.15 = f32[32]{0:T(128)S(1)} all-reduce(f32[32]{0:T(128)S(1)} %reduce_max.19), channel_id=1, replica_groups=mesh['variant'=8,'vocab'=16] {'vocab'}, use_global_device_ids=true, to_apply=%region_8.9 | all-reduce | flops 32 | bytes 256 | tf_op jit(solution)/shard_map/pmax | solution.py:46
  114.7 151.1 %all-gather.3.cloned.1.call-done = bf16[8,256,4096]{1,2,0:T(8,128)(2,1)} async-done(((bf16[8,256,32]{1,2,0:T(8,128)(2,1)}), bf16[8,256,4096]{1,2,0:T(8,128)(2,1)}) %all-gather.3.cloned.1.call-update) | async-done | bytes 16777232 | tf_op jit(solution)/shard_map/all_gather | solution.py:25
  265.9 14.8 %fusion.10 = (f32[8,256]{1,0:T(8,128)S(1)}, f32[8,256,501]{1,2,0:T(8,128)}) fusion(f32[8]{0:T(128)S(1)} %select_reduce_fusion, bf16[8,256,4096]{1,2,0:T(8,128)(2,1)} %all-gather.3.cloned.1.call-done, bf16[4096,501]{0,1:T(8,128)(2,1)} %param.9), kind=kOutput, calls=%fused_computation.23 | convolution fusion | flops 8407435264 | bytes 24993824 | tf_op jit(solution)/shard_map/vtd,dc->vtc/dot_general | solution.py:27
  280.6 62.0 %pmax.14 = f32[8,256]{1,0:T(8,128)S(1)} all-reduce(f32[8,256]{1,0:T(8,128)S(1)} %get-tuple-element.7), channel_id=1, replica_groups=mesh['variant'=8,'vocab'=16] {'variant','vocab'}, use_global_device_ids=true, to_apply=%region_2.3 | all-reduce | flops 2048 | bytes 16384 | tf_op jit(solution)/shard_map/pmax | solution.py:31
  342.6 2.7 fusion.2
  345.4 64.6 %psum.28 = f32[8,256]{1,0:T(8,128)S(1)} all-reduce(f32[8,256]{1,0:T(8,128)S(1)} %fusion.2), channel_id=1, replica_groups=mesh['variant'=8,'vocab'=16] {'variant','vocab'}, use_global_device_ids=true, to_apply=%region_4.5 | all-reduce | flops 2048 | bytes 16384 | tf_op jit(solution)/shard_map/psum | solution.py:32
  410.0 2.9 divide_reduce_fusion
  412.9 0.0 copy-start.2
  413.0 0.8 copy.13
  413.8 3.4 all-to-all-start
  417.3 0.0 all-gather.5.cloned.1.call-start
  417.3 0.3 exponential_reduce_fusion
  417.6 34.1 %psum.29 = f32[32]{0:T(128)S(1)} all-reduce(f32[32]{0:T(128)S(1)} %exponential_reduce_fusion), channel_id=1, replica_groups=mesh['variant'=8,'vocab'=16] {'vocab'}, use_global_device_ids=true, to_apply=%region_10.11 | all-reduce | flops 32 | bytes 256 | tf_op jit(solution)/shard_map/psum | solution.py:47
  451.7 0.1 convert_bitcast_fusion
  451.8 1.1 copy.14
  452.9 1.4 reshape.27
  454.2 1.1 multiply_reduce_fusion
  455.4 0.0 all-gather.5.cloned.1.call-update
  455.4 33.7 %all-reduce = (f32[32]{0:T(128)S(1)}, f32[32]{0:T(128)S(1)}) all-reduce(f32[32]{0:T(128)S(1)} %get-tuple-element.3, f32[32]{0:T(128)S(1)} %get-tuple-element.2), channel_id=1, replica_groups=mesh['variant'=8,'vocab'=16] {'vocab'}, use_global_device_ids=true, to_apply=%region_14.15 | all-reduce | flops 64 | bytes 512 | tf_op jit(solution)/shard_map/psum | solution.py:54
  489.1 0.5 subtract_multiply_fusion
  489.6 4.4 all-gather.5.cloned.1.call-done
  494.0 4.3 convolution_bitcast_fusion
  (16 shorter events, 0.1 us)
Async XLA Ops:
  8.0 1.6 copy-start
  8.0 5.8 %copy-start.5 = (f32[14]{0:T(128)S(1)}, f32[14]{0:T(128)}, u32[]{:S(2)}) copy-start(f32[14]{0:T(128)} %param.11) | copy-start | bytes 172
  8.0 5.8 %copy-start.6 = (s32[8]{0:T(128)S(1)}, s32[8]{0:T(128)}, u32[]{:S(2)}) copy-start(s32[8]{0:T(128)} %param.10) | copy-start | bytes 100
  8.0 5.9 %copy-start.4 = (s32[32]{0:T(128)S(1)}, s32[32]{0:T(128)}, u32[]{:S(2)}) copy-start(s32[32]{0:T(128)} %param.15) | copy-start | bytes 388
  8.0 66.6 %reduce-scatter.2.cloned.1.call-start = ((), (), s32[]{:S(2)}) async-start(), calls=%async_computation.3 | async-start | bytes 4718592 | tf_op jit(solution)/shard_map/reduce_scatter | solution.py:39
  13.2 252.7 %all-gather.3.cloned.1.call-start = ((), (), s32[]{:S(2)}) async-start(), calls=%async_computation.2 | async-start | bytes 16908288 | tf_op jit(solution)/shard_map/all_gather | solution.py:25
  345.4 71.9 %copy-start.1 = (f32[32,4008]{1,0:T(8,128)S(1)}, f32[32,4008]{1,0:T(8,128)}, u32[]{:S(2)}) copy-start(f32[32,4008]{1,0:T(8,128)} %reduce-scatter.2.cloned.1.call-done) | copy-start | bytes 1539076
  410.0 44.2 %copy-start.3 = (s32[32]{0:T(128)S(1)}, s32[32]{0:T(128)}, u32[]{:S(2)}) copy-start(s32[32]{0:T(128)} %param.14) | copy-start | bytes 388
  412.9 81.1 %copy-start.2 = (bf16[256,256]{1,0:T(8,128)(2,1)S(1)}, bf16[256,256]{1,0:T(8,128)(2,1)}, u32[]{:S(2)}) copy-start(bf16[256,256]{1,0:T(8,128)(2,1)} %param.12) | copy-start | bytes 393220
  413.8 37.9 %all-to-all-start = ((bf16[8,32,501]{2,1,0:T(8,128)(2,1)}), bf16[8,32,501]{2,1,0:T(8,128)(2,1)S(1)}, u32[]{:S(2)}, u32[]{:S(2)}) async-start(bf16[8,32,501]{2,1,0:T(8,128)(2,1)} %bitcast.1), calls=%async_computation | async-start | bytes 524288 | tf_op jit(solution)/shard_map/all_to_all | solution.py:35
  417.3 76.8 %all-gather.5.cloned.1.call-start = ((), (), s32[]{:S(2)}) async-start(), calls=%async_computation.4 | async-start | bytes 2359296 | tf_op jit(solution)/shard_map/all_gather | solution.py:68
Sparse Core Ops, SparseCore 0:
  13.3 61.2 reduce-scatter.1
  455.5 38.4 all-gather.4
Sparse Core Ops, SparseCore 1:
  15.4 250.4 all-gather.2
where the time goes:
time: 506 us
  blocking collectives  233 us (46%)
  waiting for transfers between devices  217 us (43%)
  matrix products  22.7 us (4%)
  between operations  15.6 us (3%)
  other arithmetic  9.06 us (2%)
    all_gather x1, waiting for transfers between devices, on_device(): lax.all_gather(teacher_hidden, ('variant', 'vocab'), axis=2, tiled=True)  151 us
    psum x1, blocking collectives, on_device(): lax.psum(jnp.sum(jnp.exp(scaled - top[:, :, None]), axis=2), ('variant',...  64.6 us
    pmax x1, blocking collectives, on_device(): top = lax.pmax(local_max, ('variant', 'vocab'))  62 us
    reduce_scatter x1, waiting for transfers between devices, on_device(): lax.psum_scatter(jnp.dot(block, student_weight, preferred_element_type=jn...  60.6 us
    pmax x1, blocking collectives, on_device(): top = lax.pmax(local_max, 'vocab')  38.9 us
    psum x1, blocking collectives, on_device(): total = lax.psum(jnp.sum(jnp.exp(logits - top[:, None]), axis=1), 'vocab')  34.1 us
    psum x1, blocking collectives, on_device(): lax.psum((jnp.sum(averaged * log_probs, axis=1), jnp.sum(jnp.where(onehot...  33.7 us
    dot_general x1, matrix products, on_device(): jnp.einsum('vtd,dc->vtc', hidden_all, teacher_weight, preferred_element_t...  14.8 us
  transfers between devices with their start and end apart: 4, of which 3 were waited for; matrix products, arithmetic and copies ran while one was open for 0% of the time, Pallas kernels for 0%

commit v1 on v0

--- a/solution.py
+++ b/solution.py
@@ -29,7 +29,9 @@
     )
     local_max = jnp.max(scaled, axis=2)
     top = lax.pmax(local_max, ("variant", "vocab"))
-    total = lax.psum(jnp.sum(jnp.exp(scaled - top[:, :, None]), axis=2), ("variant", "vocab"))
+    total = lax.psum(
+        lax.psum(jnp.sum(jnp.exp(scaled - top[:, :, None]), axis=2), "variant"), "vocab"
+    )
     probs = jnp.exp(scaled - top[:, :, None]) / total[:, :, None]
     averaged_cols = jnp.sum(probs, axis=0) / n_variant
     averaged = lax.all_to_all(

time: 506 us -> 465 us (0.919)
  blocking collectives: 233 us -> 187 us
    psum x2, blocking collectives: 98.7 us -> 52.3 us  [the longest x1 34.1 us: on_device(): lax.psum(lax.psum(jnp.sum(jnp.exp(scaled - top[:, :, None]), axis=2), 'va...]
    all_to_all x1, waiting for transfers between devices: 0.01 us -> 7.36 us  [on_device(): lax.all_to_all(averaged_cols.astype(jnp.bfloat16), 'variant', split_axis=...]
  transfers between devices with their start and end apart: 4 -> 4, of which waited for: 3 -> 4; matrix products, arithmetic and copies ran while one was open for 0% -> 1% of each run, Pallas kernels for 0% -> 0%
where the time goes in v1:
time: 465 us
  waiting for transfers between devices  221 us (48%)
  blocking collectives  187 us (40%)
  matrix products  22.7 us (5%)
  between operations  15.7 us (3%)
  other arithmetic  10.1 us (2%)
  local copies, waits for them, and re-layouts  4.83 us (1%)
    all_gather x1, waiting for transfers between devices, on_device(): lax.all_gather(teacher_hidden, ('variant', 'vocab'), axis=2, tiled=True)  150 us
    pmax x1, blocking collectives, on_device(): top = lax.pmax(local_max, ('variant', 'vocab'))  62.3 us
    reduce_scatter x1, waiting for transfers between devices, on_device(): lax.psum_scatter(jnp.dot(block, student_weight, preferred_element_type=jn...  60.6 us
    pmax x1, blocking collectives, on_device(): top = lax.pmax(local_max, 'vocab')  38.9 us
    psum x1, blocking collectives, on_device(): lax.psum(lax.psum(jnp.sum(jnp.exp(scaled - top[:, :, None]), axis=2), 'va...  34.1 us
    psum x1, blocking collectives, on_device(): lax.psum((jnp.sum(averaged * log_probs, axis=1), jnp.sum(jnp.where(onehot...  33.5 us
    psum x1, blocking collectives, on_device(): lax.psum(jnp.sum(jnp.exp(scaled - top[:, :, None]), axis=2), 'variant')  18.2 us
    dot_general x1, matrix products, on_device(): jnp.einsum('vtd,dc->vtc', hidden_all, teacher_weight, preferred_element_t...  14.8 us
  transfers between devices with their start and end apart: 4, of which 4 were waited for; matrix products, arithmetic and copies ran while one was open for 1% of the time, Pallas kernels for 0%

profile of v1, /device:TPU:0, one launch (start us, length us, event | category | flops | bytes accessed | tf_op | source)
XLA Modules:
  0.0 464.5 jit_solution(9619066202160707379)
XLA Ops:
  8.0 0.0 copy-start
  8.0 0.0 reduce-scatter.2.cloned.1.call-start
  8.1 1.5 copy-done
  9.6 3.6 fusion.11
  13.2 0.0 reduce-scatter.2.cloned.1.call-update
  13.2 0.0 all-gather.3.cloned.1.call-start
  13.2 0.5 all-gather.3.cloned.1.call-update
  13.8 0.2 select_reduce_fusion
  14.0 60.6 %reduce-scatter.2.cloned.1.call-done = f32[32,4008]{1,0:T(8,128)} async-done(((f32[256,4008]{1,0:T(8,128)}), f32[32,4008]{1,0:T(8,128)}) %reduce-scatter.2.cloned.1.call-update) | async-done | bytes 513040 | tf_op jit(solution)/shard_map/reduce_scatter | solution.py:41
  74.6 1.2 reduce_max.19
  75.8 38.9 %pmax.15 = f32[32]{0:T(128)S(1)} all-reduce(f32[32]{0:T(128)S(1)} %reduce_max.19), channel_id=1, replica_groups=mesh['variant'=8,'vocab'=16] {'vocab'}, use_global_device_ids=true, to_apply=%region_9.10 | all-reduce | flops 32 | bytes 256 | tf_op jit(solution)/shard_map/pmax | solution.py:48
  114.7 1.3 exponential_reduce_fusion
  116.0 149.5 %all-gather.3.cloned.1.call-done = bf16[8,256,4096]{1,2,0:T(8,128)(2,1)} async-done(((bf16[8,256,32]{1,2,0:T(8,128)(2,1)}), bf16[8,256,4096]{1,2,0:T(8,128)(2,1)}) %all-gather.3.cloned.1.call-update) | async-done | bytes 16777232 | tf_op jit(solution)/shard_map/all_gather | solution.py:25
  265.5 14.8 %fusion.10 = (f32[8,256]{1,0:T(8,128)S(1)}, f32[8,256,501]{1,2,0:T(8,128)}) fusion(f32[8]{0:T(128)S(1)} %select_reduce_fusion, bf16[8,256,4096]{1,2,0:T(8,128)(2,1)} %all-gather.3.cloned.1.call-done, bf16[4096,501]{0,1:T(8,128)(2,1)} %param.9), kind=kOutput, calls=%fused_computation.23 | convolution fusion | flops 8407435264 | bytes 24993824 | tf_op jit(solution)/shard_map/vtd,dc->vtc/dot_general | solution.py:27
  280.3 62.3 %pmax.14 = f32[8,256]{1,0:T(8,128)S(1)} all-reduce(f32[8,256]{1,0:T(8,128)S(1)} %get-tuple-element.9), channel_id=1, replica_groups=mesh['variant'=8,'vocab'=16] {'variant','vocab'}, use_global_device_ids=true, to_apply=%region_2.3 | all-reduce | flops 2048 | bytes 16384 | tf_op jit(solution)/shard_map/pmax | solution.py:31
  342.6 2.7 fusion.2
  345.3 18.2 %psum.35 = f32[8,256]{1,0:T(8,128)S(1)} all-reduce(f32[8,256]{1,0:T(8,128)S(1)} %fusion.2), channel_id=1, replica_groups=mesh['variant'=8,'vocab'=16] {'variant'}, use_global_device_ids=true, to_apply=%region_4.5 | all-reduce | flops 2048 | bytes 16384 | tf_op jit(solution)/shard_map/psum | solution.py:33
  363.5 34.1 %all-reduce.1 = (f32[8,256]{1,0:T(8,128)S(1)}, f32[32]{0:T(128)S(1)}) all-reduce(f32[8,256]{1,0:T(8,128)S(1)} %psum.35, f32[32]{0:T(128)S(1)} %exponential_reduce_fusion), channel_id=1, replica_groups=mesh['variant'=8,'vocab'=16] {'vocab'}, use_global_device_ids=true, to_apply=%region_5.6 | all-reduce | flops 2080 | bytes 16640 | tf_op jit(solution)/shard_map/psum | solution.py:32
  397.7 0.0 copy-start.3
  397.7 3.0 divide_reduce_fusion
  400.7 0.8 copy.13
  401.6 3.4 all-to-all-start
  405.0 0.0 all-gather.5.cloned.1.call-start
  405.1 7.4 %all-to-all-done = bf16[8,32,501]{2,1,0:T(8,128)(2,1)S(1)} async-done(((bf16[8,32,501]{2,1,0:T(8,128)(2,1)}), bf16[8,32,501]{2,1,0:T(8,128)(2,1)S(1)}, u32[]{:S(2)}, u32[]{:S(2)}) %all-to-all-start) | async-done | bytes 256544 | tf_op jit(solution)/shard_map/all_to_all | solution.py:37
  412.5 1.1 copy.14
  413.6 1.4 reshape.27
  415.0 1.1 multiply_reduce_fusion
  416.1 0.0 all-gather.5.cloned.1.call-update
  416.1 33.5 %all-reduce = (f32[32]{0:T(128)S(1)}, f32[32]{0:T(128)S(1)}) all-reduce(f32[32]{0:T(128)S(1)} %get-tuple-element.3, f32[32]{0:T(128)S(1)} %get-tuple-element.2), channel_id=1, replica_groups=mesh['variant'=8,'vocab'=16] {'vocab'}, use_global_device_ids=true, to_apply=%region_15.16 | all-reduce | flops 64 | bytes 512 | tf_op jit(solution)/shard_map/psum | solution.py:56
  449.6 0.5 subtract_multiply_fusion
  450.1 2.6 all-gather.5.cloned.1.call-done
  452.8 4.3 convolution_bitcast_fusion
  (16 shorter events, 0.1 us)
Async XLA Ops:
  8.0 1.6 copy-start
  8.0 5.7 %copy-start.5 = (f32[14]{0:T(128)S(1)}, f32[14]{0:T(128)}, u32[]{:S(2)}) copy-start(f32[14]{0:T(128)} %param.11) | copy-start | bytes 172
  8.0 5.7 %copy-start.6 = (s32[8]{0:T(128)S(1)}, s32[8]{0:T(128)}, u32[]{:S(2)}) copy-start(s32[8]{0:T(128)} %param.10) | copy-start | bytes 100
  8.0 5.9 %copy-start.4 = (s32[32]{0:T(128)S(1)}, s32[32]{0:T(128)}, u32[]{:S(2)}) copy-start(s32[32]{0:T(128)} %param.15) | copy-start | bytes 388
  8.0 66.6 %reduce-scatter.2.cloned.1.call-start = ((), (), s32[]{:S(2)}) async-start(), calls=%async_computation.3 | async-start | bytes 4718592 | tf_op jit(solution)/shard_map/reduce_scatter | solution.py:41
  13.2 252.4 %all-gather.3.cloned.1.call-start = ((), (), s32[]{:S(2)}) async-start(), calls=%async_computation.2 | async-start | bytes 16908288 | tf_op jit(solution)/shard_map/all_gather | solution.py:25
  397.6 17.3 %copy-start.1 = (f32[32,4008]{1,0:T(8,128)S(1)}, f32[32,4008]{1,0:T(8,128)}, u32[]{:S(2)}) copy-start(f32[32,4008]{1,0:T(8,128)} %reduce-scatter.2.cloned.1.call-done) | copy-start | bytes 1539076
  397.7 17.3 %copy-start.3 = (s32[32]{0:T(128)S(1)}, s32[32]{0:T(128)}, u32[]{:S(2)}) copy-start(s32[32]{0:T(128)} %param.14) | copy-start | bytes 388
  400.6 52.1 %copy-start.2 = (bf16[256,256]{1,0:T(8,128)(2,1)S(1)}, bf16[256,256]{1,0:T(8,128)(2,1)}, u32[]{:S(2)}) copy-start(bf16[256,256]{1,0:T(8,128)(2,1)} %param.12) | copy-start | bytes 393220
  401.6 10.9 %all-to-all-start = ((bf16[8,32,501]{2,1,0:T(8,128)(2,1)}), bf16[8,32,501]{2,1,0:T(8,128)(2,1)S(1)}, u32[]{:S(2)}, u32[]{:S(2)}) async-start(bf16[8,32,501]{2,1,0:T(8,128)(2,1)} %bitcast.1), calls=%async_computation | async-start | bytes 524288 | tf_op jit(solution)/shard_map/all_to_all | solution.py:37
  405.0 47.8 %all-gather.5.cloned.1.call-start = ((), (), s32[]{:S(2)}) async-start(), calls=%async_computation.4 | async-start | bytes 2359296 | tf_op jit(solution)/shard_map/all_gather | solution.py:70
Sparse Core Ops, SparseCore 0:
  13.3 61.2 reduce-scatter.1
  416.2 36.4 all-gather.4
Sparse Core Ops, SparseCore 1:
  15.4 250.1 all-gather.2
